TPU v7x, 32 devices: a whole 2x2x4 slice. The times are simulated.
32 devices in a mesh: wide: 4 (over z), narrow: 8 (over y, x, core).
Axes of the slice: x: 2, y: 2, z: 4, core: 2. Of those that a mesh axis runs over, the one named last changes fastest.
Arguments:
- kernel: bfloat16 [2048, 2048], P('wide', 'narrow'), may hold values from -0.15625 to 0.15625
- hamiltonian: bfloat16 [2048, 2048], P('wide', 'narrow'), may hold values from -6 to 6
- kernel_tiles: int32 [32, 32], P('wide', 'narrow'), may hold values from 0 to 1, as said below
- ham_tiles: int32 [32, 32], P('wide', 'narrow'), may hold values from 0 to 1, as said below
- pair_row: int32 [2048], P(('wide', 'narrow')), may hold values from 0 to 7
- pair_col: int32 [2048], P(('wide', 'narrow')), may hold values from 0 to 3
- sphere_phi: bfloat16 [2048, 64, 512], P(('wide', 'narrow')), may hold values from -0.09375 to 0.09375
- owner: int32 [8, 4], P('narrow'), may hold values from 0 to 3, each once within a row
Outputs:
- gradient: float32 [32, 64, 512], P(('wide', 'narrow'))
Inputs may be any that keep to these rules, and one draw needn't show every extreme that they name: Each row of owner is a permutation of 0 to 3. `kernel_tiles`: in each tile row, at most 4 ones fall among one narrow index's 4 tile columns, and some row has that many. `ham_tiles`: in each tile column, at most 7 ones fall among one wide index's 8 tile rows, and some column has that many.
All inputs are finite; a program needn't handle non-finite values.
Results may differ from a plain program's by a relative error of at most 0.0029.
Values may be sent and summed in bfloat16 or wider, within the bound.
A program may use at most 128 MiB of HBM per device.

v0:
```python
import jax
import jax.numpy as jnp
from jax import lax
from jax.sharding import PartitionSpec as P


def expand(mask_tiles, tile_width):
    return jnp.repeat(jnp.repeat(mask_tiles, tile_width, axis=0), tile_width, axis=1)


def collect_kernel(kmasked):
    gathered = lax.all_gather(kmasked, "narrow", axis=1, tiled=True)
    return gathered


def body(kernel, hamiltonian, kernel_tiles, ham_tiles, pair_row, pair_col, sphere_phi, owner):
    tile_width = sphere_phi.shape[1]
    kmasked = kernel * expand(kernel_tiles, tile_width).astype(jnp.bfloat16)
    hmasked = hamiltonian * expand(ham_tiles, tile_width).astype(jnp.bfloat16)
    height = kernel.shape[0]
    breadth = hamiltonian.shape[1]
    kernel_full = collect_kernel(kmasked)
    coefficients = jnp.dot(
        kernel_full,
        lax.all_gather(hmasked, "wide", axis=0, tiled=True),
        preferred_element_type=jnp.float32,
    )
    coefficients = coefficients.astype(jnp.bfloat16)
    tile_rows = height // tile_width
    tile_cols = breadth // tile_width
    tile_table = coefficients.reshape(tile_rows, tile_width, tile_cols, tile_width).transpose(
        0, 2, 1, 3
    )
    tile_blocks = tile_table[pair_row, pair_col]
    gradient_blocks = jnp.einsum(
        "pij,pir->pjr", tile_blocks, sphere_phi, preferred_element_type=jnp.float32
    )
    local_owner = owner[0]
    column_ids = jnp.arange(tile_cols, dtype=jnp.int32)
    dest_slot = jnp.sum(
        jnp.where(pair_col[:, None] == column_ids[None, :], local_owner[None, :], 0), axis=1
    )
    chooser = (dest_slot[None, :] == column_ids[:, None]).astype(jnp.float32)
    partials = jnp.einsum("qp,pjr->qjr", chooser, gradient_blocks, precision=lax.Precision.HIGHEST)
    return lax.psum_scatter(partials, "wide", scatter_dimension=0, tiled=True)


def solution(mesh):
    return jax.shard_map(
        body,
        mesh=mesh,
        in_specs=(
            P("wide", "narrow"),
            P("wide", "narrow"),
            P("wide", "narrow"),
            P("wide", "narrow"),
            P(("wide", "narrow")),
            P(("wide", "narrow")),
            P(("wide", "narrow"), None, None),
            P("narrow", None),
        ),
        out_specs=P(("wide", "narrow"), None, None),
        check_vma=False,
    )
```

profile of v0, /device:TPU:0, one launch (start us, length us, event | category | flops | bytes accessed | tf_op | source)
XLA Modules:
  0.0 113.4 jit_solution(17894622116828058528)
XLA Ops:
  6.5 0.0 all-gather.5.cloned.1.call-start
  6.5 1.1 copy.23
  7.6 0.7 convert_element_type.29
  8.3 0.1 broadcast_in_dim.41
  8.4 0.1 convert_element_type.30
  8.5 0.7 bitcast_multiply_fusion
  9.2 0.0 all-gather.5.cloned.1.call-update
  9.2 0.0 all-gather.3.cloned.1.call-start
  9.3 1.1 copy.22
  10.4 0.7 convert_element_type.26
  11.1 0.1 broadcast_in_dim.39
  11.1 0.1 convert_element_type.27
  11.2 0.7 bitcast_multiply_fusion.1
  12.0 0.0 all-gather.3.cloned.1.call-update
  12.0 0.0 reduce-scatter.2.cloned.1.call-start
  12.0 0.8 select_reduce_fusion
  12.8 0.7 fusion.7
  13.5 26.6 %all-gather.5.cloned.1.call-done = bf16[2048,256]{0,1:T(8,128)(2,1)} async-done(((bf16[512,256]{0,1:T(8,128)(2,1)}), bf16[2048,256]{0,1:T(8,128)(2,1)}) %all-gather.5.cloned.1.call-update) | async-done | bytes 1048592 | tf_op jit(solution)/shard_map/all_gather | solution.py:25
  40.1 29.1 %all-gather.3.cloned.1.call-done = bf16[512,2048]{0,1:T(8,128)(2,1)} async-done(((bf16[512,256]{0,1:T(8,128)(2,1)}), bf16[512,2048]{0,1:T(8,128)(2,1)}) %all-gather.3.cloned.1.call-update) | async-done | bytes 2097168 | tf_op jit(solution)/shard_map/all_gather | solution.py:12
  69.2 2.6 %convolution_convert_fusion = bf16[512,256]{1,0:T(8,128)(2,1)S(1)} fusion(bf16[512,2048]{0,1:T(8,128)(2,1)} %all-gather.3.cloned.1.call-done, bf16[2048,256]{0,1:T(8,128)(2,1)} %all-gather.5.cloned.1.call-done), kind=kOutput, calls=%fused_computation.3 | convolution fusion | flops 537001984 | bytes 3407872 | tf_op jit(solution)/shard_map/dot_general | solution.py:23
  71.8 0.2 reshape.13
  72.0 0.1 copy.32
  72.2 0.8 gather_fusion
  73.0 3.5 %fusion.10 = f32[64,64,512]{2,1,0:T(8,128)S(1)} fusion(bf16[64,64,64]{2,1,0:T(8,128)(2,1)S(1)} %gather_fusion, bf16[64,64,512]{2,1,0:T(8,128)(2,1)} %param.14), kind=kOutput, calls=%fused_computation.19 | convolution fusion | flops 268435456 | bytes 13107200 | tf_op jit(solution)/shard_map/pij,pir->pjr/dot_general | solution.py:35
  76.5 7.5 %fusion = f32[4,64,512]{2,0,1:T(4,128)S(1)} fusion(f32[64,64,512]{2,1,0:T(8,128)S(1)} %fusion.10, s32[64]{0:T(128)S(1)} %select_reduce_fusion), kind=kOutput, calls=%fused_computation.1 | convolution fusion | flops 100663552 | bytes 8913152 | tf_op jit(solution)/shard_map/qp,pjr->qjr/dot_general | solution.py:44
  83.9 1.0 copy.27
  84.9 0.0 reduce-scatter.2.cloned.1.call-update
  84.9 22.0 %reduce-scatter.2.cloned.1.call-done = f32[1,64,512]{2,1,0:T(8,128)} async-done(((f32[4,64,512]{2,1,0:T(8,128)}), f32[1,64,512]{2,1,0:T(8,128)}) %reduce-scatter.2.cloned.1.call-update) | async-done | bytes 131088 | tf_op jit(solution)/shard_map/reduce_scatter | solution.py:45
Async XLA Ops:
  6.5 33.6 %all-gather.5.cloned.1.call-start = ((), (), s32[]{:S(2)}) async-start(), calls=%async_computation.2 | async-start | bytes 1310720 | tf_op jit(solution)/shard_map/all_gather | solution.py:25
  9.2 59.9 %all-gather.3.cloned.1.call-start = ((), (), s32[]{:S(2)}) async-start(), calls=%async_computation.1 | async-start | bytes 2359296 | tf_op jit(solution)/shard_map/all_gather | solution.py:12
  12.0 94.9 %reduce-scatter.2.cloned.1.call-start = ((), (), s32[]{:S(2)}) async-start(), calls=%async_computation.3 | async-start | bytes 655360 | tf_op jit(solution)/shard_map/reduce_scatter | solution.py:45
Sparse Core Ops, SparseCore 0:
  9.3 30.6 all-gather.4
  42.0 27.1 all-gather.2
  85.0 21.8 reduce-scatter.1
where the time goes:
time: 114 us; the launch traced here: 113 us
  waiting for transfers between devices  77.7 us (68%)
  matrix products  13.6 us (12%)
  between operations  13.2 us (12%)
  local copies, waits for them, and re-layouts  4.63 us (4%)
  other arithmetic  4.25 us (4%)
    all_gather x1, waiting for transfers between devices, collect_kernel(): gathered = lax.all_gather(kmasked, 'narrow', axis=1, tiled=True)  29.1 us
    all_gather x1, waiting for transfers between devices, body(): lax.all_gather(hmasked, 'wide', axis=0, tiled=True)  26.6 us
    reduce_scatter x1, waiting for transfers between devices, body(): return lax.psum_scatter(partials, 'wide', scatter_dimension=0, tiled=True)  22 us
    dot_general x1, matrix products, body(): jnp.einsum('qp,pjr->qjr', chooser, gradient_blocks, precision=lax.Precisi...  7.47 us
    dot_general x1, matrix products, body(): jnp.einsum('pij,pir->pjr', tile_blocks, sphere_phi, preferred_element_typ...  3.48 us
    dot_general x1, matrix products, body(): jnp.dot(kernel_full, lax.all_gather(hmasked, 'wide', axis=0, tiled=True),...  2.61 us
  transfers between devices with their start and end apart: 3, of which 3 were waited for; matrix products, arithmetic and copies ran while one was open for 4% of the time, Pallas kernels for 0%

commit v1 on v0

--- a/solution.py
+++ b/solution.py
@@ -2,6 +2,28 @@
 import jax.numpy as jnp
 from jax import lax
 from jax.sharding import PartitionSpec as P
+
+
+def in_order(tiles, dim):
+    dims = list(tiles.shape[1:])
+    dims[dim] *= tiles.shape[0]
+    return jnp.moveaxis(tiles, 0, dim).reshape(dims)
+
+
+def ring_gather(shard, axis, dim):
+    peers = lax.axis_size(axis)
+    pairs = [(i, (i + 1) % peers) for i in range(peers)]
+    back = [(b, a) for a, b in pairs]
+    lower, upper = ([], [])
+    for turn in range(peers - 1):
+        if turn % 2 == 0:
+            lower.append(lax.ppermute(lower[-1] if lower else shard, axis, pairs))
+        else:
+            upper.append(lax.ppermute(upper[-1] if upper else shard, axis, back))
+    pieces = jnp.stack([*lower[::-1], shard, *upper])
+    shift = lax.axis_index(axis) - len(lower)
+    pieces = pieces[(jnp.arange(peers) - shift) % peers]
+    return in_order(pieces, dim)
 
 
 def expand(mask_tiles, tile_width):
@@ -9,7 +31,7 @@
 
 
 def collect_kernel(kmasked):
-    gathered = lax.all_gather(kmasked, "narrow", axis=1, tiled=True)
+    gathered = ring_gather(kmasked, "narrow", 1)
     return gathered
 
 

time: 114 us -> 103 us (0.904)
  waiting for transfers between devices: 77.7 us -> 57.6 us
  starting transfers between devices: 0.09 us -> 8.72 us
  local copies, waits for them, and re-layouts: 4.63 us -> 6.84 us
  other arithmetic: 4.25 us -> 2.24 us
    all_gather x1 -> x0, waiting for transfers between devices: 29.1 us -> none  [collect_kernel(): gathered = lax.all_gather(kmasked, 'narrow', axis=1, tiled=True)]
    ppermute x0 -> x7, waiting for transfers between devices: none -> 22.4 us  [the longest x4 13.2 us: ring_gather(): lower.append(lax.ppermute(lower[-1] if lower else shard, axis, pairs))]
    all_gather x1, waiting for transfers between devices: 26.6 us -> 13.8 us  [body(): lax.all_gather(hmasked, 'wide', axis=0, tiled=True)]
    ppermute x0 -> x7, starting transfers between devices: none -> 8.67 us  [the longest x3 8.12 us: ring_gather(): upper.append(lax.ppermute(upper[-1] if upper else shard, axis, back))]
    gather x0 -> x1, local copies, waits for them, and re-layouts: none -> 2.01 us  [ring_gather(): pieces = pieces[(jnp.arange(peers) - shift) % peers]]
    unnamed x2 -> x15, local copies, waits for them, and re-layouts: 2.18 us -> 2.36 us
  transfers between devices with their start and end apart: 3 -> 9, of which waited for: 3 -> 7; matrix products, arithmetic and copies ran while one was open for 4% -> 5% of each run, Pallas kernels for 0% -> 0%
where the time goes in v1:
time: 103 us
  waiting for transfers between devices  57.6 us (56%)
  matrix products  13.6 us (13%)
  between operations  13.6 us (13%)
  starting transfers between devices  8.72 us (8%)
  local copies, waits for them, and re-layouts  6.84 us (7%)
  other arithmetic  2.24 us (2%)
    reduce_scatter x1, waiting for transfers between devices, body(): return lax.psum_scatter(partials, 'wide', scatter_dimension=0, tiled=True)  21.4 us
    all_gather x1, waiting for transfers between devices, body(): lax.all_gather(hmasked, 'wide', axis=0, tiled=True)  13.8 us
    ppermute x4, waiting for transfers between devices, ring_gather(): lower.append(lax.ppermute(lower[-1] if lower else shard, axis, pairs))  13.2 us
    ppermute x3, waiting for transfers between devices, ring_gather(): upper.append(lax.ppermute(upper[-1] if upper else shard, axis, back))  9.16 us
    ppermute x3, starting transfers between devices, ring_gather(): upper.append(lax.ppermute(upper[-1] if upper else shard, axis, back))  8.12 us
    dot_general x1, matrix products, body(): jnp.einsum('qp,pjr->qjr', chooser, gradient_blocks, precision=lax.Precisi...  7.47 us
    dot_general x1, matrix products, body(): jnp.einsum('pij,pir->pjr', tile_blocks, sphere_phi, preferred_element_typ...  3.49 us
    dot_general x1, matrix products, body(): jnp.dot(kernel_full, lax.all_gather(hmasked, 'wide', axis=0, tiled=True),...  2.6 us
  transfers between devices with their start and end apart: 9, of which 7 were waited for; matrix products, arithmetic and copies ran while one was open for 5% of the time, Pallas kernels for 0%

profile of v1, /device:TPU:0, one launch (start us, length us, event | category | flops | bytes accessed | tf_op | source)
XLA Modules:
  0.0 102.6 jit_solution(14958515649605292967)
XLA Ops:
  6.5 0.0 copy-start.2
  6.5 0.0 copy-start
  6.5 0.0 copy-start.1
  6.5 0.0 all-gather.2.cloned.1.call-start
  6.5 1.1 %copy.22 = bf16[512,256]{0,1:T(8,128)(2,1)S(1)} copy(bf16[512,256]{1,0:T(8,128)(2,1)} %param.8) | data formatting | bytes 524288 | tf_op args[0]
  7.7 0.7 convert_element_type.26
  8.4 0.1 broadcast_in_dim.40
  8.4 0.1 convert_element_type.27
  8.6 0.5 collective-permute-start
  9.1 6.9 %collective-permute-done = bf16[512,256]{0,1:T(8,128)(2,1)S(1)} collective-permute-done((bf16[512,256]{0,1:T(8,128)(2,1)S(1)}, bf16[512,256]{0,1:T(8,128)(2,1)S(1)}, u32[]{:S(2)}, u32[]{:S(2)}) %collective-permute-start) | collective-permute-done | bytes 262176 | tf_op jit(solution)/shard_map/ppermute | solution.py:20
  16.0 0.0 collective-permute-start.1
  16.0 2.6 %collective-permute-start.4 = (bf16[512,256]{0,1:T(8,128)(2,1)S(1)}, bf16[512,256]{0,1:T(8,128)(2,1)S(1)}, u32[]{:S(2)}, u32[]{:S(2)}) collective-permute-start(bf16[512,256]{0,1:T(8,128)(2,1)S(1)} %bitcast_multiply_fusion.1), channel_id=1, source_target_pairs={{1,0},{2,1},{3,2},{4,3},{5,4},{6,5},{7,6},{0,7},{9,8},{10,9},{11,1... | collective-permute-start | bytes 786440 | tf_op jit(solution)/shard_map/ppermute | solution.py:22
  18.7 5.2 %collective-permute-done.1 = bf16[512,256]{0,1:T(8,128)(2,1)S(1)} collective-permute-done((bf16[512,256]{0,1:T(8,128)(2,1)S(1)}, bf16[512,256]{0,1:T(8,128)(2,1)S(1)}, u32[]{:S(2)}, u32[]{:S(2)}) %collective-permute-start.1) | collective-permute-done | bytes 262176 | tf_op jit(solution)/shard_map/ppermute | solution.py:20
  23.8 0.0 collective-permute-start.2
  23.8 1.1 %copy.23 = bf16[512,256]{0,1:T(8,128)(2,1)S(1)} copy(bf16[512,256]{1,0:T(8,128)(2,1)} %param.9) | data formatting | bytes 524288 | tf_op args[1]
  24.9 0.7 convert_element_type.29
  25.6 0.1 broadcast_in_dim.42
  25.7 0.1 convert_element_type.30
  25.8 0.7 bitcast_multiply_fusion
  26.5 0.0 all-gather.2.cloned.1.call-update
  26.5 0.0 reduce-scatter.2.cloned.1.call-start
  26.6 0.0 copy-done.2
  26.6 0.0 copy-done
  26.6 0.1 select_reduce_fusion
  26.7 0.0 collective-permute-done.4
  26.7 2.7 %collective-permute-start.5 = (bf16[512,256]{0,1:T(8,128)(2,1)S(1)}, bf16[512,256]{0,1:T(8,128)(2,1)S(1)}, u32[]{:S(2)}, u32[]{:S(2)}) collective-permute-start(bf16[512,256]{0,1:T(8,128)(2,1)S(1)} %collective-permute-done.4), channel_id=1, source_target_pairs={{1,0},{2,1},{3,2},{4,3},{5,4},{6,5},{7,6},{0,7},{9,8},{10,9},{11,1... | collective-permute-start | bytes 786440 | tf_op jit(solution)/shard_map/ppermute | solution.py:22
  29.4 1.1 %collective-permute-done.2 = bf16[512,256]{0,1:T(8,128)(2,1)S(1)} collective-permute-done((bf16[512,256]{0,1:T(8,128)(2,1)S(1)}, bf16[512,256]{0,1:T(8,128)(2,1)S(1)}, u32[]{:S(2)}, u32[]{:S(2)}) %collective-permute-start.2) | collective-permute-done | bytes 262176 | tf_op jit(solution)/shard_map/ppermute | solution.py:20
  30.6 0.0 collective-permute-start.3
  30.6 0.0 copy-done.1
  30.6 5.5 %collective-permute-done.5 = bf16[512,256]{0,1:T(8,128)(2,1)S(1)} collective-permute-done((bf16[512,256]{0,1:T(8,128)(2,1)S(1)}, bf16[512,256]{0,1:T(8,128)(2,1)S(1)}, u32[]{:S(2)}, u32[]{:S(2)}) %collective-permute-start.5) | collective-permute-done | bytes 262176 | tf_op jit(solution)/shard_map/ppermute | solution.py:22
  36.0 2.8 %collective-permute-start.6 = (bf16[512,256]{0,1:T(8,128)(2,1)S(1)}, bf16[512,256]{0,1:T(8,128)(2,1)S(1)}, u32[]{:S(2)}, u32[]{:S(2)}) collective-permute-start(bf16[512,256]{0,1:T(8,128)(2,1)S(1)} %collective-permute-done.5), channel_id=1, source_target_pairs={{1,0},{2,1},{3,2},{4,3},{5,4},{6,5},{7,6},{0,7},{9,8},{10,9},{11,1... | collective-permute-start | bytes 786440 | tf_op jit(solution)/shard_map/ppermute | solution.py:22
  38.8 0.0 collective-permute-done.3
  39.0 3.7 %collective-permute-done.6 = bf16[512,256]{0,1:T(8,128)(2,1)S(1)} collective-permute-done((bf16[512,256]{0,1:T(8,128)(2,1)S(1)}, bf16[512,256]{0,1:T(8,128)(2,1)S(1)}, u32[]{:S(2)}, u32[]{:S(2)}) %collective-permute-start.6) | collective-permute-done | bytes 262176 | tf_op jit(solution)/shard_map/ppermute | solution.py:22
  42.8 2.0 %gather_fusion = bf16[8,512,256]{1,2,0:T(8,128)(2,1)} fusion(bf16[8,512,256]{1,2,0:T(8,128)(2,1)S(1)} %bitcast_dynamic-update-slice_fusion, s32[1024]{0:T(1024)S(1)} %pad_clamp_fusion), kind=kCustom, calls=%fused_computation | custom fusion | bytes 4194336 | tf_op jit(solution)/shard_map/gather | solution.py:25
  44.8 13.8 %all-gather.2.cloned.1.call-done = bf16[2048,256]{0,1:T(8,128)(2,1)} async-done(((bf16[512,256]{0,1:T(8,128)(2,1)}), bf16[2048,256]{0,1:T(8,128)(2,1)}) %all-gather.2.cloned.1.call-update) | async-done | bytes 1048592 | tf_op jit(solution)/shard_map/all_gather | solution.py:47
  58.6 2.6 %convolution_convert_fusion = bf16[512,256]{1,0:T(8,128)(2,1)S(1)} fusion(bf16[512,2048]{0,1:T(8,128)(2,1)} %bitcast.41, bf16[2048,256]{0,1:T(8,128)(2,1)} %all-gather.2.cloned.1.call-done), kind=kOutput, calls=%fused_computation.4 | convolution fusion | flops 537001984 | bytes 3407872 | tf_op jit(solution)/shard_map/dot_general | solution.py:45
  61.2 0.2 reshape.66
  61.5 0.1 copy.32
  61.6 0.8 gather_fusion.1
  62.4 3.5 %fusion.12 = f32[64,64,512]{2,1,0:T(8,128)S(1)} fusion(bf16[64,64,64]{2,1,0:T(8,128)(2,1)S(1)} %gather_fusion.1, bf16[64,64,512]{2,1,0:T(8,128)(2,1)} %param.14), kind=kOutput, calls=%fused_computation.35 | convolution fusion | flops 268435456 | bytes 13107200 | tf_op jit(solution)/shard_map/pij,pir->pjr/dot_general | solution.py:57
  65.9 7.5 %fusion = f32[4,64,512]{2,0,1:T(4,128)S(1)} fusion(f32[64,64,512]{2,1,0:T(8,128)S(1)} %fusion.12, s32[64]{0:T(128)S(1)} %select_reduce_fusion), kind=kOutput, calls=%fused_computation.2 | convolution fusion | flops 100663552 | bytes 8913152 | tf_op jit(solution)/shard_map/qp,pjr->qjr/dot_general | solution.py:66
  73.4 1.0 copy.27
  74.3 0.0 reduce-scatter.2.cloned.1.call-update
  74.3 21.4 %reduce-scatter.2.cloned.1.call-done = f32[1,64,512]{2,1,0:T(8,128)} async-done(((f32[4,64,512]{2,1,0:T(8,128)}), f32[1,64,512]{2,1,0:T(8,128)}) %reduce-scatter.2.cloned.1.call-update) | async-done | bytes 131088 | tf_op jit(solution)/shard_map/reduce_scatter | solution.py:67
  (12 shorter events, 0.2 us)
Async XLA Ops:
  6.5 20.1 %copy-start.2 = (s32[64]{0:T(128)S(1)}, s32[64]{0:T(128)}, u32[]{:S(2)}) copy-start(s32[64]{0:T(128)} %param.13) | copy-start | bytes 772
  6.5 20.1 %copy-start = (s32[1,4]{1,0:T(1,128)S(1)}, s32[1,4]{1,0:T(1,128)}, u32[]{:S(2)}) copy-start(s32[1,4]{1,0:T(1,128)} %param.15) | copy-start | bytes 52
  6.5 24.0 %copy-start.1 = (s32[64]{0:T(128)S(1)}, s32[64]{0:T(128)}, u32[]{:S(2)}) copy-start(s32[64]{0:T(128)} %param.12) | copy-start | bytes 772
  6.5 52.1 %all-gather.2.cloned.1.call-start = ((), (), s32[]{:S(2)}) async-start(), calls=%async_computation.1 | async-start | bytes 1310720 | tf_op jit(solution)/shard_map/all_gather | solution.py:47
  8.6 7.5 %collective-permute-start = (bf16[512,256]{0,1:T(8,128)(2,1)S(1)}, bf16[512,256]{0,1:T(8,128)(2,1)S(1)}, u32[]{:S(2)}, u32[]{:S(2)}) collective-permute-start(bf16[512,256]{0,1:T(8,128)(2,1)S(1)} %bitcast_multiply_fusion.1), channel_id=1, source_target_pairs={{0,1},{1,2},{2,3},{3,4},{4,5},{5,6},{6,7},{7,0},{8,9},{9,10},{10,1... | collective-permute-start | bytes 786440 | tf_op jit(solution)/shard_map/ppermute | solution.py:20
  16.0 7.8 %collective-permute-start.1 = (bf16[512,256]{0,1:T(8,128)(2,1)S(1)}, bf16[512,256]{0,1:T(8,128)(2,1)S(1)}, u32[]{:S(2)}, u32[]{:S(2)}) collective-permute-start(bf16[512,256]{0,1:T(8,128)(2,1)S(1)} %collective-permute-done), channel_id=1, source_target_pairs={{0,1},{1,2},{2,3},{3,4},{4,5},{5,6},{6,7},{7,0},{8,9},{9,10},{10,1... | collective-permute-start | bytes 786440 | tf_op jit(solution)/shard_map/ppermute | solution.py:20
  16.0 10.7 %collective-permute-start.4 = (bf16[512,256]{0,1:T(8,128)(2,1)S(1)}, bf16[512,256]{0,1:T(8,128)(2,1)S(1)}, u32[]{:S(2)}, u32[]{:S(2)}) collective-permute-start(bf16[512,256]{0,1:T(8,128)(2,1)S(1)} %bitcast_multiply_fusion.1), channel_id=1, source_target_pairs={{1,0},{2,1},{3,2},{4,3},{5,4},{6,5},{7,6},{0,7},{9,8},{10,9},{11,1... | collective-permute-start | bytes 786440 | tf_op jit(solution)/shard_map/ppermute | solution.py:22
  23.8 6.7 %collective-permute-start.2 = (bf16[512,256]{0,1:T(8,128)(2,1)S(1)}, bf16[512,256]{0,1:T(8,128)(2,1)S(1)}, u32[]{:S(2)}, u32[]{:S(2)}) collective-permute-start(bf16[512,256]{0,1:T(8,128)(2,1)S(1)} %collective-permute-done.1), channel_id=1, source_target_pairs={{0,1},{1,2},{2,3},{3,4},{4,5},{5,6},{6,7},{7,0},{8,9},{9,10},{10,1... | collective-permute-start | bytes 786440 | tf_op jit(solution)/shard_map/ppermute | solution.py:20
  26.5 69.2 %reduce-scatter.2.cloned.1.call-start = ((), (), s32[]{:S(2)}) async-start(), calls=%async_computation.2 | async-start | bytes 655360 | tf_op jit(solution)/shard_map/reduce_scatter | solution.py:67
  26.7 9.3 %collective-permute-start.5 = (bf16[512,256]{0,1:T(8,128)(2,1)S(1)}, bf16[512,256]{0,1:T(8,128)(2,1)S(1)}, u32[]{:S(2)}, u32[]{:S(2)}) collective-permute-start(bf16[512,256]{0,1:T(8,128)(2,1)S(1)} %collective-permute-done.4), channel_id=1, source_target_pairs={{1,0},{2,1},{3,2},{4,3},{5,4},{6,5},{7,6},{0,7},{9,8},{10,9},{11,1... | collective-permute-start | bytes 786440 | tf_op jit(solution)/shard_map/ppermute | solution.py:22
  30.6 8.3 %collective-permute-start.3 = (bf16[512,256]{0,1:T(8,128)(2,1)S(1)}, bf16[512,256]{0,1:T(8,128)(2,1)S(1)}, u32[]{:S(2)}, u32[]{:S(2)}) collective-permute-start(bf16[512,256]{0,1:T(8,128)(2,1)S(1)} %collective-permute-done.2), channel_id=1, source_target_pairs={{0,1},{1,2},{2,3},{3,4},{4,5},{5,6},{6,7},{7,0},{8,9},{9,10},{10,1... | collective-permute-start | bytes 786440 | tf_op jit(solution)/shard_map/ppermute | solution.py:20
  36.0 6.7 %collective-permute-start.6 = (bf16[512,256]{0,1:T(8,128)(2,1)S(1)}, bf16[512,256]{0,1:T(8,128)(2,1)S(1)}, u32[]{:S(2)}, u32[]{:S(2)}) collective-permute-start(bf16[512,256]{0,1:T(8,128)(2,1)S(1)} %collective-permute-done.5), channel_id=1, source_target_pairs={{1,0},{2,1},{3,2},{4,3},{5,4},{6,5},{7,6},{0,7},{9,8},{10,9},{11,1... | collective-permute-start | bytes 786440 | tf_op jit(solution)/shard_map/ppermute | solution.py:22
Sparse Core Ops, SparseCore 0:
  26.7 31.8 all-gather.1
  74.5 21.2 reduce-scatter.1
